TPU v7x, 128 devices: a whole 4x4x4 slice. The times are simulated.
128 devices in a mesh: batch: 8 (over y_lo, x), corpus: 16 (over z, y_hi, core).
Axes of the slice: x: 4, y: 4 (y_hi: 2, y_lo: 2; y = y_hi * 2 + y_lo), z: 4, core: 2. Of those that a mesh axis runs over, the one named last changes fastest.
Arguments:
- states: bfloat16 [8192, 4096], P('batch', 'corpus'), may hold values from -6 to 6
- norm_gain: float32 [4096], replicated, may hold values from 0.25 to 1.75
- gate_weight: bfloat16 [4096, 12288], P('batch', 'corpus'), may hold values from -0.09375 to 0.09375
- up_weight: bfloat16 [4096, 12288], P('batch', 'corpus'), may hold values from -0.09375 to 0.09375
- down_weight: bfloat16 [12288, 4096], P('corpus', 'batch'), may hold values from -0.0546875 to 0.0546875
- final_gain: float32 [4096], replicated, may hold values from 0.25 to 1.75
- hash_weight: bfloat16 [4096, 1024], replicated, may hold values from -0.75 to 0.75
- query_bits: bfloat16 [4096, 1024], replicated, may hold values from -1 to 1
- slot_map: int32 [128], replicated, may hold values from 0 to 127, each once
- query_index: int32 [4096, 100], replicated, may hold values from 0 to 127
Outputs:
- scores: float32 [4096, 100], P(('batch', 'corpus'))
Inputs may be any that keep to these rules, and one draw needn't show every extreme that they name: `slot_map`: each corpus entry is named by exactly one document.
All inputs are finite; a program needn't handle non-finite values.
Results may differ from a plain program's by a relative error of at most 0.017.
Values may be sent and summed in bfloat16 or wider, within the bound.
No kernel may reach another device: no remote copies, remote signals or barrier semaphores. Data moves between devices by JAX's collectives and lax.ppermute only.
A program may use at most 192 MiB of HBM per device.

v0:
```python
import jax
import jax.numpy as jnp
from jax import lax
from jax.sharding import PartitionSpec as P

DOC_LEN = 64
CODE = 1024
NQ = 4096


def side_by_side(arrays, axis, dim, along):
    both = jnp.concatenate(arrays, axis=along)
    whole, at, gathered = (lax.all_gather(both, axis, axis=dim, tiled=True), 0, [])
    for a in arrays:
        gathered.append(lax.slice_in_dim(whole, at, at + a.shape[along], axis=along))
        at += a.shape[along]
    return tuple(gathered)


def rms(values, gain):
    return values * lax.rsqrt(jnp.mean(values * values, axis=-1, keepdims=True) + 1e-06) * gain


def add_rows(left, piece):
    return jnp.dot(left, piece, preferred_element_type=jnp.float32)


def local(
    states,
    norm_gain,
    gate_weight,
    up_weight,
    down_weight,
    final_gain,
    hash_weight,
    query_bits,
    slot_map,
    query_index,
):
    corpus_count = lax.axis_size("corpus")
    devices = lax.axis_size("batch") * corpus_count
    flat_index = lax.axis_index("batch") * corpus_count + lax.axis_index("corpus")
    whole = lax.all_gather(states, "corpus", axis=1, tiled=True)
    normed = rms(whole.astype(jnp.float32), norm_gain).astype(jnp.bfloat16)
    pieces = side_by_side((gate_weight, up_weight), "batch", 0, 1)
    gate = add_rows(normed, pieces[0])
    up = add_rows(normed, pieces[1])
    hidden = (jax.nn.silu(gate) * up).astype(jnp.bfloat16)
    terms = jnp.dot(
        hidden,
        lax.all_gather(down_weight, "batch", axis=1, tiled=True),
        preferred_element_type=jnp.float32,
    )
    ffn = lax.psum_scatter(
        terms.astype(jnp.bfloat16), "corpus", scatter_dimension=0, tiled=True
    ).astype(jnp.float32)
    own_rows = ffn.shape[0]
    mine = lax.dynamic_slice_in_dim(whole, lax.axis_index("corpus") * own_rows, own_rows, 0)
    resid = mine.astype(jnp.float32) + ffn
    finals = rms(resid, final_gain)
    owned_docs = own_rows // DOC_LEN
    pooled = jnp.mean(finals.reshape(owned_docs, DOC_LEN, finals.shape[1]), axis=1).astype(
        jnp.bfloat16
    )
    codes = jnp.tanh(jnp.dot(pooled, hash_weight, preferred_element_type=jnp.float32)).astype(
        jnp.bfloat16
    )
    doc_total = owned_docs * devices
    scale = 1.0 / jnp.sqrt(jnp.float32(CODE))
    gathered = lax.all_gather(codes, ("batch", "corpus"), axis=0, tiled=True)
    placing = (slot_map[:, None] == jnp.arange(doc_total, dtype=jnp.int32)[None, :]).astype(
        jnp.bfloat16
    )
    corpus = jnp.einsum("ds,dc->sc", placing, gathered, preferred_element_type=jnp.float32).astype(
        jnp.bfloat16
    )
    query_rows = NQ // devices
    my_bits = lax.dynamic_slice_in_dim(query_bits, flat_index * query_rows, query_rows, 0)
    my_index = lax.dynamic_slice_in_dim(query_index, flat_index * query_rows, query_rows, 0)
    table = jnp.dot(my_bits, corpus.T, preferred_element_type=jnp.float32) * scale
    scores = jnp.take_along_axis(table, my_index, axis=1)
    return scores


def solution(mesh):
    placed = (
        P("batch", "corpus"),
        P(),
        P("batch", "corpus"),
        P("batch", "corpus"),
        P("corpus", "batch"),
        P(),
        P(),
        P(),
        P(),
        P(),
    )
    return jax.shard_map(
        local, mesh=mesh, in_specs=placed, out_specs=P(("batch", "corpus"), None), check_vma=False
    )
```

profile of v0, /device:TPU:1, one launch (start us, length us, event | category | flops | bytes accessed | tf_op | source)
XLA Modules:
  0.0 631.7 jit_solution(1051141560968313369)
XLA Ops:
  6.5 0.7 all-gather.5.cloned.1.call-update
  7.3 2.7 pad_maximum_fusion
  10.0 0.0 all-gather.9.cloned.1.call-start
  10.1 0.7 all-gather.9.cloned.1.call-update
  10.7 0.0 reduce-scatter.2.cloned.1.call-start
  10.8 79.1 %all-gather.5.cloned.1.call-done = bf16[1024,4096]{1,0:T(8,128)(2,1)} async-done(((bf16[1024,256]{1,0:T(8,128)(2,1)}), bf16[1024,4096]{1,0:T(8,128)(2,1)}) %all-gather.5.cloned.1.call-update) | async-done | bytes 8388624 | tf_op jit(solution)/shard_map/all_gather | solution.py:43
  89.9 5.1 fusion
  95.0 124.5 %all-gather.7.cloned.1.call-done = bf16[4096,1536]{1,0:T(8,128)(2,1)} async-done(((bf16[512,1536]{1,0:T(8,128)(2,1)}), bf16[4096,1536]{1,0:T(8,128)(2,1)}) %all-gather.7.cloned.1.call-update) | async-done | bytes 12582928 | tf_op jit(solution)/shard_map/all_gather | solution.py:13
  219.5 12.4 %fusion.3 = f32[1024,768]{1,0:T(8,128)} fusion(bf16[4096,1536]{1,0:T(8,128)(2,1)} %all-gather.7.cloned.1.call-done, bf16[1024,4096]{1,0:T(8,128)(2,1)} %all-gather.5.cloned.1.call-done, f32[4096]{0:T(1024)S(1)} %copy-done.3, f32[1024]{0:T(1024)S(1)} %add_rsqrt_fusion), kind=kOutput, calls=%fused_computation.7 | convolution fusion | flops 6459228160 | bytes 17846272 | tf_op jit(solution)/shard_map/dot_general | solution.py:25
  231.9 60.2 %all-gather.9.cloned.1.call-done = bf16[768,4096]{1,0:T(8,128)(2,1)} async-done(((bf16[768,512]{1,0:T(8,128)(2,1)}), bf16[768,4096]{1,0:T(8,128)(2,1)}) %all-gather.9.cloned.1.call-update) | async-done | bytes 6291472 | tf_op jit(solution)/shard_map/all_gather | solution.py:51
  292.1 26.3 %convolution_convert_fusion = bf16[1024,4096]{1,0:T(8,128)(2,1)} fusion(bf16[768,4096]{1,0:T(8,128)(2,1)} %all-gather.9.cloned.1.call-done, f32[1024,768]{1,0:T(8,128)} %fusion.3, bf16[4096,1536]{1,0:T(8,128)(2,1)} %all-gather.7.cloned.1.call-done, bf16[1024,4096]{1,0:T(8,128)(2,1)} %all-gather.5.cloned.1.call-done, f32[4096]{0:T(1024)S(1)} %copy-done.3, ...), kind=kOutput, calls=%fused_computation.6 | convolution fusion | flops 12910592000 | bytes 32526336 | tf_op jit(solution)/shard_map/dot_general | solution.py:49
  318.4 0.1 constant_dynamic-slice_fusion
  318.5 0.1 copy.14
  318.6 0.1 reshape.40
  318.7 99.8 %reduce-scatter.2.cloned.1.call-done = bf16[64,4096]{1,0:T(8,128)(2,1)} async-done(((bf16[1024,4096]{1,0:T(8,128)(2,1)}), bf16[64,4096]{1,0:T(8,128)(2,1)}) %reduce-scatter.2.cloned.1.call-update) | async-done | bytes 524304 | tf_op jit(solution)/shard_map/reduce_scatter | solution.py:54
  418.5 1.5 multiply_reduce_fusion.1
  420.0 1.5 multiply_reduce_fusion
  421.5 4.6 fusion.25
  426.1 177.8 %all-gather = bf16[131072]{0:T(1024)(128)(2,1)S(1)} all-gather(bf16[1024]{0:T(1024)(128)(2,1)S(1)} %tanh_convert_fusion), channel_id=2, replica_groups=mesh['batch'=8,'corpus'=16] {'batch','corpus'}, dimensions={0}, use_global_device_ids=true | all-gather | bytes 264192 | tf_op jit(solution)/shard_map/all_gather | solution.py:70
  603.9 0.1 reshape.46
  604.1 1.3 fusion.19
  605.4 19.0 %gather_fusion = f32[3200]{0:T(1024)S(1)} fusion(f32[32,128]{1,0:T(8,128)S(1)} %fusion.19, s32[3200]{0:T(1024)S(1)} %reshape.40), kind=kCustom, calls=%fused_computation | custom fusion | bytes 51200 | tf_op jit(solution)/shard_map/jit(take_along_axis)/gather | solution.py:81
  624.4 0.1 reshape.43
  624.5 0.6 and_select_fusion
  (18 shorter events, 0.1 us)
Async XLA Ops:
  6.5 311.9 %copy-start = (s32[4096,100]{0,1:T(8,128)S(1)}, s32[4096,100]{0,1:T(8,128)}, u32[]{:S(2)}) copy-start(s32[4096,100]{0,1:T(8,128)} %param.19) | copy-start | bytes 4915204
  6.5 83.3 %all-gather.5.cloned.1.call-start = ((), (), s32[]{:S(2)}) async-start(), calls=%async_computation.1 | async-start | bytes 8912896 | tf_op jit(solution)/shard_map/all_gather | solution.py:43
  7.3 212.2 %copy-start.3 = (f32[4096]{0:T(1024)S(1)}, f32[4096]{0:T(1024)}, u32[]{:S(2)}) copy-start(f32[4096]{0:T(1024)} %param.11) | copy-start | bytes 49156
  7.3 212.2 %all-gather.7.cloned.1.call-start = ((), (), s32[]{:S(2)}) async-start(), calls=%async_computation.2 | async-start | bytes 14155776 | tf_op jit(solution)/shard_map/all_gather | solution.py:13
  10.0 282.1 %all-gather.9.cloned.1.call-start = ((), (), s32[]{:S(2)}) async-start(), calls=%async_computation.3 | async-start | bytes 7077888 | tf_op jit(solution)/shard_map/all_gather | solution.py:51
  10.7 407.8 %reduce-scatter.2.cloned.1.call-start = ((), (), s32[]{:S(2)}) async-start(), calls=%async_computation.4 | async-start | bytes 8912896 | tf_op jit(solution)/shard_map/reduce_scatter | solution.py:54
  318.4 101.6 %copy-start.1 = (f32[4096]{0:T(1024)S(1)}, f32[4096]{0:T(1024)}, u32[]{:S(2)}) copy-start(f32[4096]{0:T(1024)} %param.15) | copy-start | bytes 49156
  421.5 182.6 %copy-start.2 = (s32[128]{0:T(128)S(1)}, s32[128]{0:T(128)}, u32[]{:S(2)}) copy-start(s32[128]{0:T(128)} %param.18) | copy-start | bytes 1540
Sparse Core Ops, SparseCore 0:
  9.7 80.1 all-gather.4
  91.5 127.9 all-gather.6
  221.1 70.9 all-gather.8
  318.5 99.9 reduce-scatter.1
where the time goes:
time: 632 us
  waiting for transfers between devices  365 us (58%)
  blocking collectives  178 us (28%)
  matrix products  44.6 us (7%)
  local copies, waits for them, and re-layouts  19.5 us (3%)
  between operations  13.2 us (2%)
  other arithmetic  11.3 us (2%)
    all_gather x1, blocking collectives, local(): gathered = lax.all_gather(codes, ('batch', 'corpus'), axis=0, tiled=True)  178 us
    all_gather x1, waiting for transfers between devices, side_by_side(): lax.all_gather(both, axis, axis=dim, tiled=True)  125 us
    reduce_scatter x1, waiting for transfers between devices, local(): lax.psum_scatter(terms.astype(jnp.bfloat16), 'corpus', scatter_dimension=...  99.8 us
    all_gather x1, waiting for transfers between devices, local(): whole = lax.all_gather(states, 'corpus', axis=1, tiled=True)  79.1 us
    all_gather x1, waiting for transfers between devices, local(): lax.all_gather(down_weight, 'batch', axis=1, tiled=True)  60.2 us
    dot_general x1, matrix products, local(): jnp.dot(hidden, lax.all_gather(down_weight, 'batch', axis=1, tiled=True),...  26.3 us
    gather x3, local copies, waits for them, and re-layouts, local(): scores = jnp.take_along_axis(table, my_index, axis=1)  19.2 us
  transfers between devices with their start and end apart: 4, of which 4 were waited for; matrix products, arithmetic and copies ran while one was open for 3% of the time, Pallas kernels for 0%

commit v1 on v0

--- a/solution.py
+++ b/solution.py
@@ -67,18 +67,19 @@
     )
     doc_total = owned_docs * devices
     scale = 1.0 / jnp.sqrt(jnp.float32(CODE))
-    gathered = lax.all_gather(codes, ("batch", "corpus"), axis=0, tiled=True)
-    placing = (slot_map[:, None] == jnp.arange(doc_total, dtype=jnp.int32)[None, :]).astype(
-        jnp.bfloat16
-    )
-    corpus = jnp.einsum("ds,dc->sc", placing, gathered, preferred_element_type=jnp.float32).astype(
-        jnp.bfloat16
+    gathered = lax.all_to_all(
+        jnp.broadcast_to(codes[:, None], (owned_docs, devices, CODE)).reshape(doc_total, CODE),
+        ("batch", "corpus"),
+        0,
+        0,
+        tiled=True,
     )
     query_rows = NQ // devices
     my_bits = lax.dynamic_slice_in_dim(query_bits, flat_index * query_rows, query_rows, 0)
     my_index = lax.dynamic_slice_in_dim(query_index, flat_index * query_rows, query_rows, 0)
-    table = jnp.dot(my_bits, corpus.T, preferred_element_type=jnp.float32) * scale
-    scores = jnp.take_along_axis(table, my_index, axis=1)
+    table = jnp.dot(my_bits, gathered.T, preferred_element_type=jnp.float32) * scale
+    chosen = my_index[:, :, None] == slot_map[None, None, :]
+    scores = jnp.sum(jnp.where(chosen, table[:, None, :], 0.0), axis=-1)
     return scores
 
 

time: 632 us -> 460 us (0.73)
  blocking collectives: 178 us -> 0 us
  local copies, waits for them, and re-layouts: 19.5 us -> 2.69 us
  waiting for transfers between devices: 365 us -> 376 us
  starting transfers between devices: 0.12 us -> 8.52 us
    all_gather x1 -> x0, blocking collectives: 178 us -> none  [local(): gathered = lax.all_gather(codes, ('batch', 'corpus'), axis=0, tiled=True)]
    gather x3 -> x0, local copies, waits for them, and re-layouts: 19.2 us -> none  [local(): scores = jnp.take_along_axis(table, my_index, axis=1)]
    all_to_all x0 -> x1, waiting for transfers between devices: none -> 10.9 us  [local(): lax.all_to_all(jnp.broadcast_to(codes[:, None], (owned_docs, devices, COD...]
    all_to_all x0 -> x1, starting transfers between devices: none -> 8.4 us  [local(): lax.all_to_all(jnp.broadcast_to(codes[:, None], (owned_docs, devices, COD...]
  transfers between devices with their start and end apart: 4 -> 5, of which waited for: 4 -> 5; matrix products, arithmetic and copies ran while one was open for 3% -> 4% of each run, Pallas kernels for 0% -> 0%
where the time goes in v1:
time: 460 us; the launch traced here: 459 us
  waiting for transfers between devices  376 us (82%)
  matrix products  44.3 us (10%)
  other arithmetic  14.2 us (3%)
  between operations  13.2 us (3%)
  starting transfers between devices  8.52 us (2%)
    all_gather x1, waiting for transfers between devices, side_by_side(): lax.all_gather(both, axis, axis=dim, tiled=True)  125 us
    reduce_scatter x1, waiting for transfers between devices, local(): lax.psum_scatter(terms.astype(jnp.bfloat16), 'corpus', scatter_dimension=...  100 us
    all_gather x1, waiting for transfers between devices, local(): whole = lax.all_gather(states, 'corpus', axis=1, tiled=True)  79.1 us
    all_gather x1, waiting for transfers between devices, local(): lax.all_gather(down_weight, 'batch', axis=1, tiled=True)  60.3 us
    dot_general x1, matrix products, local(): jnp.dot(hidden, lax.all_gather(down_weight, 'batch', axis=1, tiled=True),...  26.4 us
    dot_general x1, matrix products, add_rows(): return jnp.dot(left, piece, preferred_element_type=jnp.float32)  12.4 us
    all_to_all x1, waiting for transfers between devices, local(): lax.all_to_all(jnp.broadcast_to(codes[:, None], (owned_docs, devices, COD...  10.9 us
  transfers between devices with their start and end apart: 5, of which 5 were waited for; matrix products, arithmetic and copies ran while one was open for 4% of the time, Pallas kernels for 0%

profile of v1, /device:TPU:1, one launch (start us, length us, event | category | flops | bytes accessed | tf_op | source)
XLA Modules:
  0.0 459.3 jit_solution(606428503006756444)
XLA Ops:
  6.5 0.7 all-gather.4.cloned.1.call-update
  7.3 2.7 pad_maximum_fusion
  10.0 0.7 all-gather.8.cloned.1.call-update
  10.8 79.1 %all-gather.4.cloned.1.call-done = bf16[1024,4096]{1,0:T(8,128)(2,1)} async-done(((bf16[1024,256]{1,0:T(8,128)(2,1)}), bf16[1024,4096]{1,0:T(8,128)(2,1)}) %all-gather.4.cloned.1.call-update) | async-done | bytes 8388624 | tf_op jit(solution)/shard_map/all_gather | solution.py:43
  89.9 5.1 %fusion = f32[1024]{0:T(1024)S(1)} fusion(bf16[1024,4096]{1,0:T(8,128)(2,1)} %all-gather.4.cloned.1.call-done), kind=kLoop, calls=%fused_computation.2 | loop fusion | flops 12581888 | bytes 8392704 | tf_op jit(solution)/shard_map/reduce_sum | solution.py:21
  95.0 124.5 %all-gather.6.cloned.1.call-done = bf16[4096,1536]{1,0:T(8,128)(2,1)} async-done(((bf16[512,1536]{1,0:T(8,128)(2,1)}), bf16[4096,1536]{1,0:T(8,128)(2,1)}) %all-gather.6.cloned.1.call-update) | async-done | bytes 12582928 | tf_op jit(solution)/shard_map/all_gather | solution.py:13
  219.5 12.4 %fusion.3 = f32[1024,768]{1,0:T(8,128)} fusion(bf16[4096,1536]{1,0:T(8,128)(2,1)} %all-gather.6.cloned.1.call-done, bf16[1024,4096]{1,0:T(8,128)(2,1)} %all-gather.4.cloned.1.call-done, f32[4096]{0:T(1024)S(1)} %copy-done.3, f32[1024]{0:T(1024)S(1)} %add_rsqrt_fusion), kind=kOutput, calls=%fused_computation.6 | convolution fusion | flops 6459228160 | bytes 17846272 | tf_op jit(solution)/shard_map/dot_general | solution.py:25
  231.8 60.3 %all-gather.8.cloned.1.call-done = bf16[768,4096]{1,0:T(8,128)(2,1)} async-done(((bf16[768,512]{1,0:T(8,128)(2,1)}), bf16[768,4096]{1,0:T(8,128)(2,1)}) %all-gather.8.cloned.1.call-update) | async-done | bytes 6291472 | tf_op jit(solution)/shard_map/all_gather | solution.py:51
  292.1 26.4 %convolution_convert_fusion = bf16[1024,4096]{1,0:T(8,128)(2,1)} fusion(bf16[768,4096]{1,0:T(8,128)(2,1)} %all-gather.8.cloned.1.call-done, f32[1024,768]{1,0:T(8,128)} %fusion.3, bf16[4096,1536]{1,0:T(8,128)(2,1)} %all-gather.6.cloned.1.call-done, bf16[1024,4096]{1,0:T(8,128)(2,1)} %all-gather.4.cloned.1.call-done, f32[4096]{0:T(1024)S(1)} %copy-done.3, ...), kind=kOutput, calls=%fused_computation.5 | convolution fusion | flops 12910592000 | bytes 32526336 | tf_op jit(solution)/shard_map/dot_general | solution.py:49
  318.5 100.1 %reduce-scatter.2.cloned.1.call-done = bf16[64,4096]{1,0:T(8,128)(2,1)} async-done(((bf16[1024,4096]{1,0:T(8,128)(2,1)}), bf16[64,4096]{1,0:T(8,128)(2,1)}) %reduce-scatter.2.cloned.1.call-update) | async-done | bytes 524304 | tf_op jit(solution)/shard_map/reduce_scatter | solution.py:54
  418.6 1.5 multiply_reduce_fusion.1
  420.1 1.5 multiply_reduce_fusion
  421.6 4.6 fusion.23
  426.2 0.3 reshape.44
  426.5 0.5 broadcast.38
  427.0 2.3 reduce.2
  429.3 0.9 reshape.47
  430.1 8.4 %all-to-all-start = ((bf16[128,2,512]{2,1,0:T(2,128)(2,1)}), bf16[128,2,512]{2,1,0:T(2,128)(2,1)S(1)}, u32[]{:S(2)}, u32[]{:S(2)}) async-start(bf16[128,2,512]{2,1,0:T(2,128)(2,1)} %reshape.47), calls=%async_computation.1 | async-start | bytes 524288 | tf_op jit(solution)/shard_map/all_to_all | solution.py:70
  438.5 0.1 constant_dynamic-slice_fusion
  438.6 10.9 %all-to-all-done = bf16[128,2,512]{2,1,0:T(2,128)(2,1)S(1)} async-done(((bf16[128,2,512]{2,1,0:T(2,128)(2,1)}), bf16[128,2,512]{2,1,0:T(2,128)(2,1)S(1)}, u32[]{:S(2)}, u32[]{:S(2)}) %all-to-all-start) | async-done | bytes 262176 | tf_op jit(solution)/shard_map/all_to_all | solution.py:70
  449.6 0.2 reshape.48
  449.8 1.0 convolution_multiply_fusion
  450.8 1.3 select_reduce_fusion
  452.1 0.7 copy.14
  (19 shorter events, 0.2 us)
Async XLA Ops:
  6.5 432.0 %copy-start = (s32[4096,100]{0,1:T(8,128)S(1)}, s32[4096,100]{0,1:T(8,128)}, u32[]{:S(2)}) copy-start(s32[4096,100]{0,1:T(8,128)} %param.19) | copy-start | bytes 4915204
  6.5 212.9 %copy-start.3 = (f32[4096]{0:T(1024)S(1)}, f32[4096]{0:T(1024)}, u32[]{:S(2)}) copy-start(f32[4096]{0:T(1024)} %param.11) | copy-start | bytes 49156
  6.5 83.3 %all-gather.4.cloned.1.call-start = ((), (), s32[]{:S(2)}) async-start(), calls=%async_computation.2 | async-start | bytes 8912896 | tf_op jit(solution)/shard_map/all_gather | solution.py:43
  7.3 212.2 %all-gather.6.cloned.1.call-start = ((), (), s32[]{:S(2)}) async-start(), calls=%async_computation.3 | async-start | bytes 14155776 | tf_op jit(solution)/shard_map/all_gather | solution.py:13
  10.0 282.1 %all-gather.8.cloned.1.call-start = ((), (), s32[]{:S(2)}) async-start(), calls=%async_computation.4 | async-start | bytes 7077888 | tf_op jit(solution)/shard_map/all_gather | solution.py:51
  10.7 407.9 %reduce-scatter.2.cloned.1.call-start = ((), (), s32[]{:S(2)}) async-start(), calls=%async_computation.5 | async-start | bytes 8912896 | tf_op jit(solution)/shard_map/reduce_scatter | solution.py:54
  318.5 101.6 %copy-start.1 = (f32[4096]{0:T(1024)S(1)}, f32[4096]{0:T(1024)}, u32[]{:S(2)}) copy-start(f32[4096]{0:T(1024)} %param.15) | copy-start | bytes 49156
  421.6 29.2 %copy-start.2 = (s32[128]{0:T(128)S(1)}, s32[128]{0:T(128)}, u32[]{:S(2)}) copy-start(s32[128]{0:T(128)} %param.18) | copy-start | bytes 1540
  430.1 19.4 %all-to-all-start = ((bf16[128,2,512]{2,1,0:T(2,128)(2,1)}), bf16[128,2,512]{2,1,0:T(2,128)(2,1)S(1)}, u32[]{:S(2)}, u32[]{:S(2)}) async-start(bf16[128,2,512]{2,1,0:T(2,128)(2,1)} %reshape.47), calls=%async_computation.1 | async-start | bytes 524288 | tf_op jit(solution)/shard_map/all_to_all | solution.py:70
Sparse Core Ops, SparseCore 0:
  9.7 80.1 all-gather.3
  91.5 127.9 all-gather.5
  221.1 70.9 all-gather.7
  318.6 99.9 reduce-scatter.1
